TPU v7x, 512 devices: a whole 4x8x8 slice. The times are simulated.
512 devices in a mesh: dp: 16 (over y, core), ctx: 32 (over z, x).
Axes of the slice: x: 4, y: 8, z: 8, core: 2. Of those that a mesh axis runs over, the one named last changes fastest.
Arguments:
- delta_query_rows: bfloat16 [16, 4096, 16, 128], P('dp', 'ctx'), may hold values from -6 to 6
- delta_key_rows: bfloat16 [16, 4096, 16, 128], P('dp', 'ctx'), may hold values from -6 to 6
- delta_value_rows: bfloat16 [16, 4096, 16, 128], P('dp', 'ctx'), may hold values from -6 to 6
- delta_write_strength: float32 [16, 4096, 16], P('dp', 'ctx'), may hold values from 0.2 to 1
- token_gate_scale: float32 [16, 4096, 16], P('dp', 'ctx'), may hold values from 0.5 to 2
- channel_decay_rate: float32 [16, 128], replicated, may hold values from 0.00390625 to 0.0625
- sudden_loss_mask: int32 [16, 4096], P('dp', 'ctx'), may hold values 0 or 1
- document_numbers: int32 [16, 4096], P('dp'), may hold values from 0 to 63, never falling along the last dimension, each value on 1 to 128 neighbouring positions
- delta_norm_gain: float32 [128], replicated, may hold values from 0.5 to 1.5
- delta_output_cotangent: bfloat16 [16, 4096, 16, 128], P('dp', 'ctx'), may hold values from -6 to 6
- latent_query_rows: bfloat16 [16, 4096, 16, 128], P('dp', 'ctx'), may hold values from -90 to 90
- compressed_latents: bfloat16 [16, 4096, 512], P('dp', 'ctx'), may hold values from -90 to 90
- query_to_latent_map: bfloat16 [16, 128, 512], P(None, 'ctx'), may hold values from -0.5 to 0.5
- latent_to_value_map: bfloat16 [16, 512, 128], P(None, 'ctx'), may hold values from -0.25 to 0.25
Outputs:
- kda_output: bfloat16 [16, 4096, 16, 128], P('dp', 'ctx')
- mla_output: bfloat16 [16, 4096, 16, 128], P('dp', 'ctx')
- gain_grad: float32 [128], replicated
Inputs may be any that keep to these rules, and one draw needn't show every extreme that they name: `document_numbers`: each row's document numbers never fall; every document has 1 to 128 tokens, and some document has exactly 128.
All inputs are finite; a program needn't handle non-finite values. No bound on the sum of `sudden_loss_mask` on one device may be relied on, other than what follows from the above.
Results may differ from a plain program's by a relative error of at most 0.0065.
The roundings to bfloat16 on the way count: a program that leaves them out, or rounds other values in their place, can miss the bound.
Values may be sent and summed in bfloat16 or wider, within the bound.
No kernel may reach another device: no remote copies, remote signals or barrier semaphores. Data moves between devices by JAX's collectives and lax.ppermute only.
A program may use at most 128 MiB of HBM per device.

v0:
```python
import math
import jax
import jax.numpy as jnp
from jax import lax
from jax.sharding import PartitionSpec as P

DOCBLK = 2
DN = 128
exact_mode = lax.Precision.HIGHEST


def from_behind(value, axis, steps):
    count = lax.axis_size(axis)
    leading, last = (max(0, -steps), min(count, count - steps))
    return lax.ppermute(value, axis, [(source, source + steps) for source in range(leading, last)])


def unit_norm(tensor):
    widened = tensor.astype(jnp.float32)
    return widened * lax.rsqrt(jnp.sum(widened * widened, axis=-1, keepdims=True) + 1e-06)


def block_maps(queries, keyset, values, writes, log_decay_values, docs, before):
    size = docs.shape[0]
    places = jnp.arange(size, dtype=jnp.int32)
    same_doc = docs[:, None] == docs[None, :]
    within = (same_doc & (places[:, None] >= places[None, :])).astype(jnp.float32)
    earlier = (same_doc & (places[:, None] > places[None, :])).astype(jnp.float32)
    cumlog = jnp.einsum("ts,shc->thc", within, log_decay_values, precision=exact_mode)
    key_decayed = keyset * jnp.exp(cumlog)
    key_grown = keyset * jnp.exp(-cumlog)
    query_decayed = queries * jnp.exp(cumlog)
    carried = (docs == before).astype(jnp.float32)
    pairwise = jnp.einsum("thc,shc->hts", key_decayed, key_grown, precision=exact_mode)
    triangle = pairwise * jnp.transpose(writes)[:, :, None] * earlier[None]
    targets = jnp.concatenate(
        [writes[:, :, None] * values, (writes * carried[:, None])[:, :, None] * key_decayed],
        axis=-1,
    )
    identity_mat = jnp.eye(size, dtype=jnp.float32)
    solved = jax.scipy.linalg.solve_triangular(
        identity_mat[None] + triangle,
        jnp.transpose(targets, (1, 0, 2)),
        lower=True,
        unit_diagonal=True,
    )
    value_width = values.shape[-1]
    from_values = solved[:, :, :value_width]
    from_state = solved[:, :, value_width:]
    weights_att = (
        jnp.einsum("thc,shc->hts", query_decayed, key_grown, precision=exact_mode) * within[None]
    )
    local_out = jnp.einsum("hts,hsv->thv", weights_att, from_values, precision=exact_mode)
    state_query = carried[:, None, None] * query_decayed - jnp.einsum(
        "hts,hsc->thc", weights_att, from_state, precision=exact_mode
    )
    closing = jnp.exp(cumlog[size - 1])
    tailing = (docs == docs[size - 1]).astype(jnp.float32)
    leaving = key_grown * closing[None] * tailing[:, None, None]
    key_width = keyset.shape[-1]
    transfer_map = (carried[size - 1] * closing)[:, :, None] * jnp.eye(
        key_width, dtype=jnp.float32
    )[None]
    transfer_map = transfer_map - jnp.einsum(
        "shc,hsd->hcd", leaving, from_state, precision=exact_mode
    )
    offset_map = jnp.einsum("shc,hsv->hcv", leaving, from_values, precision=exact_mode)
    return (local_out, state_query, transfer_map, offset_map)


def advance(transfer_map, offset_map, state):
    return jnp.einsum("shcd,shdv->shcv", transfer_map, state, precision=exact_mode) + offset_map


def shards(
    delta_query_rows,
    delta_key_rows,
    delta_value_rows,
    delta_write_strength,
    token_gate_scale,
    channel_decay_rate,
    sudden_loss_mask,
    document_numbers,
    delta_norm_gain,
    delta_output_cotangent,
    latent_query_rows,
    compressed_latents,
    query_to_latent_map,
    latent_to_value_map,
):
    ranks = lax.axis_size("ctx")
    place = lax.axis_index("ctx")
    seqs = delta_query_rows.shape[0]
    rows = delta_query_rows.shape[1]
    half = rows // 2
    heads = delta_query_rows.shape[2]
    key_width = delta_query_rows.shape[3]
    value_width = delta_value_rows.shape[3]
    second_block = 2 * ranks - 1 - place
    zero_index = jnp.zeros((), jnp.int32)

    def block_docs(block):
        start = block * half
        docs = lax.dynamic_slice_in_dim(document_numbers, start, half, 1)
        prior = lax.dynamic_slice_in_dim(document_numbers, jnp.maximum(start - 1, 0), 1, 1)[:, 0]
        return (docs, jnp.where(block > 0, prior, -1))

    docs_first, prior_first = block_docs(place)
    docs_second, prior_second = block_docs(second_block)
    docs_pair = jnp.stack([docs_first, docs_second], axis=1)
    prior_pair = jnp.stack([prior_first, prior_second], axis=1)

    def split_rows(tensor):
        return tensor.reshape((seqs, 2, half) + tensor.shape[2:])

    queries = split_rows(unit_norm(delta_query_rows))
    keyset = split_rows(unit_norm(delta_key_rows))
    values = split_rows(delta_value_rows.astype(jnp.float32))
    writes = split_rows(delta_write_strength)
    log_decay_values = split_rows(
        -channel_decay_rate[None, None] * token_gate_scale[..., None]
        + sudden_loss_mask.astype(jnp.float32)[:, :, None, None] * math.log(0.6)
    )
    local_out, state_query, transfer_map, offset_map = jax.vmap(jax.vmap(block_maps))(
        queries, keyset, values, writes, log_decay_values, docs_pair, prior_pair
    )
    zero_state = jnp.zeros((seqs, heads, key_width, value_width), jnp.float32)
    state_first = zero_state
    state_second = zero_state
    for repeat in range(DOCBLK):
        out_first = advance(transfer_map[:, 0], offset_map[:, 0], state_first)
        out_second = advance(transfer_map[:, 1], offset_map[:, 1], state_second)
        state_first = from_behind(out_first, "ctx", 1)
        from_above = from_behind(out_second, "ctx", -1)
        state_second = jnp.where(place == ranks - 1, out_first, from_above)
    states = jnp.stack([state_first, state_second], axis=1)
    kda_raw = local_out + jnp.einsum(
        "sbthc,sbhcv->sbthv", state_query, states, precision=exact_mode
    )
    kda_raw = kda_raw.reshape(seqs, rows, heads, value_width)
    meansq = jnp.mean(kda_raw * kda_raw, axis=-1, keepdims=True)
    normed = kda_raw * lax.rsqrt(meansq + 1e-06)
    kda_output = (normed * delta_norm_gain).astype(jnp.bfloat16)
    partial_grad = jnp.sum(normed * delta_output_cotangent.astype(jnp.float32), axis=(0, 1, 2))
    total_grad = lax.psum(partial_grad, ("dp", "ctx"))
    gain_grad = total_grad / math.sqrt(seqs * lax.axis_size("dp") * rows * ranks * heads)
    latent_width = compressed_latents.shape[2]
    neighbours = {0: compressed_latents}
    offsets = []
    for distance in range(1, DOCBLK + 1):
        offsets.append(distance)
        offsets.append(-distance)
    for offset in offsets:
        neighbours[offset] = from_behind(compressed_latents, "ctx", offset)
    stacked = jnp.stack([neighbours[offset] for offset in range(-DOCBLK, DOCBLK + 1)], axis=0)
    stacked = stacked.reshape(2 * DOCBLK + 1, seqs, 2, half, latent_width)
    lift_keys, lift_values = (
        lax.all_gather(query_to_latent_map, "ctx", axis=1, tiled=True),
        lax.all_gather(latent_to_value_map, "ctx", axis=1, tiled=True),
    )
    lifted = jnp.einsum(
        "sthn,hnl->sthl", latent_query_rows, lift_keys, preferred_element_type=jnp.float32
    ).astype(jnp.bfloat16)
    scale = 1.0 / math.sqrt(DN)
    halves_out = []
    for which in range(2):
        block = place if which == 0 else second_block
        key_parts = []
        doc_parts = []
        pos_parts = []
        for back in range(DOCBLK, -1, -1):
            source = block - back
            in_first = source < ranks
            owner = jnp.where(in_first, source, 2 * ranks - 1 - source)
            side = jnp.where(in_first, 0, 1).astype(jnp.int32)
            slot = jnp.clip(place - owner, -DOCBLK, DOCBLK) + DOCBLK
            piece = lax.dynamic_slice(
                stacked,
                (slot, zero_index, side, zero_index, zero_index),
                (1, seqs, 1, half, latent_width),
            )
            key_parts.append(piece.reshape(seqs, half, latent_width))
            source_docs = lax.dynamic_slice_in_dim(
                document_numbers, jnp.maximum(source, 0) * half, half, 1
            )
            doc_parts.append(jnp.where(source >= 0, source_docs, -1))
            pos_parts.append(source * half + jnp.arange(half, dtype=jnp.int32))
        key_rows = jnp.concatenate(key_parts, axis=1)
        key_docs = jnp.concatenate(doc_parts, axis=1)
        key_pos = jnp.concatenate(pos_parts, axis=0)
        query_docs = docs_pair[:, which]
        query_pos = block * half + jnp.arange(half, dtype=jnp.int32)
        block_query = lifted[:, which * half : (which + 1) * half]
        logits = (
            jnp.einsum("sthl,skl->shtk", block_query, key_rows, preferred_element_type=jnp.float32)
            * scale
        )
        allowed = (query_docs[:, None, :, None] == key_docs[:, None, None, :]) & (
            key_pos[None, None, None, :] <= query_pos[None, None, :, None]
        )
        logits = jnp.where(allowed, logits, -jnp.inf)
        peak = jnp.max(logits, axis=-1, keepdims=True)
        expo = jnp.exp(logits - peak)
        probs = (expo / jnp.sum(expo, axis=-1, keepdims=True)).astype(jnp.bfloat16)
        latent_mix = jnp.einsum(
            "shtk,skl->sthl", probs, key_rows, preferred_element_type=jnp.float32
        ).astype(jnp.bfloat16)
        halves_out.append(
            jnp.einsum(
                "sthl,hlv->sthv", latent_mix, lift_values, preferred_element_type=jnp.float32
            ).astype(jnp.bfloat16)
        )
    mla_output = jnp.concatenate(halves_out, axis=1)
    return (kda_output, mla_output, gain_grad)


def solution(mesh):
    placed = (
        P("dp", "ctx", None, None),
        P("dp", "ctx", None, None),
        P("dp", "ctx", None, None),
        P("dp", "ctx", None),
        P("dp", "ctx", None),
        P(),
        P("dp", "ctx"),
        P("dp", None),
        P(),
        P("dp", "ctx", None, None),
        P("dp", "ctx", None, None),
        P("dp", "ctx", None),
        P(None, "ctx", None),
        P(None, "ctx", None),
    )
    return jax.shard_map(
        shards,
        mesh=mesh,
        in_specs=placed,
        out_specs=(P("dp", "ctx", None, None), P("dp", "ctx", None, None), P()),
        check_vma=False,
    )
```

profile of v0, /device:TPU:1, one launch (start us, length us, event | category | flops | bytes accessed | tf_op | source)
XLA Modules:
  0.0 411.5 jit_solution(6213377689688391206)
XLA Ops:
  7.2 1.4 collective-permute-start.5
  8.7 1.3 collective-permute-start.4
  10.0 7.0 %collective-permute-start.7 = (bf16[1,128,512]{2,1,0:T(8,128)(2,1)}, bf16[1,128,512]{2,1,0:T(8,128)(2,1)S(1)}, u32[]{:S(2)}, u32[]{:S(2)}) collective-permute-start(bf16[1,128,512]{2,1,0:T(8,128)(2,1)} %param.25), channel_id=1, source_target_pairs={{0,2},{1,3},{2,4},{3,5},{4,6},{5,7},{6,8},{7,9},{8,10},{9,11},{10,... | collective-permute-start | bytes 393224 | tf_op jit(solution)/shard_map/ppermute | solution.py:15
  16.9 1.5 copy.62
  18.6 1.5 broadcast_select_fusion.5
  20.1 0.2 slice_reduce_fusion
  20.3 0.7 iota_compare_fusion.5
  21.0 1.3 constant_dynamic-slice_fusion.7
  23.5 0.7 compare_convert_fusion
  24.2 0.7 multiply_reduce_fusion.2
  24.9 0.8 mul.321
  25.6 0.8 reshape.779
  26.4 0.1 mul.313
  26.5 0.7 neg.8
  27.2 0.8 mul.308
  28.0 1.1 convert.6
  29.1 0.3 fusion.36
  29.5 0.1 fusion.71
  29.6 0.9 fusion.42
  30.5 0.3 convert_multiply_fusion.2
  30.9 1.5 multiply_bitcast_fusion
  32.4 3.1 fusion.27
  35.4 158.9 %custom-call.4 = f32[1,2,16,1,64,64]{4,5,3,2,1,0:T(8,128)} custom-call(f32[1,2,16,1,64,64]{5,4,3,2,1,0:T(8,128)} %fusion.27), custom_call_target="InvertDiagBlocksLowerTriangular" | custom-call | tf_op jit(solution)/shard_map/vmap(vmap(jit(_solve_triangular)))/vmap()/triangular_solve | solution.py:41
  194.4 0.9 broadcast_compare_fusion
  195.2 0.2 fusion.77
  195.4 0.4 copy_multiply_fusion.1
  195.9 2.0 fusion.10
  198.0 3.6 convolution_bitcast_fusion
  201.6 4.0 subtract_bitcast_fusion
  205.6 2.0 fusion.20
  207.7 1.9 collective-permute-start.2
  209.6 2.0 fusion.22
  211.6 5.0 %collective-permute-start = (f32[1,16,128,128]{3,2,1,0:T(8,128)}, f32[1,16,128,128]{3,2,1,0:T(8,128)}, u32[]{:S(2)}, u32[]{:S(2)}) collective-permute-start(f32[1,16,128,128]{3,2,1,0:T(8,128)} %fusion.22), channel_id=1, source_target_pairs={{0,1},{1,2},{2,3},{3,4},{4,5},{5,6},{6,7},{7,8},{8,9},{9,10},{10,1... | collective-permute-start | bytes 3145736 | tf_op jit(solution)/shard_map/ppermute | solution.py:15
  216.7 0.3 fusion.37
  217.1 0.3 convert_multiply_fusion
  217.6 2.1 convolution_multiply_fusion.2
  219.8 0.1 compare_and_fusion.3
  219.9 1.1 fusion.45
  221.0 1.5 fusion.29
  222.5 5.7 %collective-permute-done.2 = f32[1,16,128,128]{3,2,1,0:T(8,128)} collective-permute-done((f32[1,16,128,128]{3,2,1,0:T(8,128)}, f32[1,16,128,128]{3,2,1,0:T(8,128)}, u32[]{:S(2)}, u32[]{:S(2)}) %collective-permute-start.2) | collective-permute-done | bytes 1048608 | tf_op jit(solution)/shard_map/ppermute | solution.py:15
  228.2 3.5 fusion.19
  231.7 1.4 collective-permute-start.3
  233.1 2.4 fusion.21
  235.5 5.8 %collective-permute-start.1 = (f32[1,16,128,128]{3,2,1,0:T(8,128)S(1)}, f32[1,16,128,128]{3,2,1,0:T(8,128)}, u32[]{:S(2)}, u32[]{:S(2)}) collective-permute-start(f32[1,16,128,128]{3,2,1,0:T(8,128)S(1)} %fusion.21), channel_id=1, source_target_pairs={{0,1},{1,2},{2,3},{3,4},{4,5},{5,6},{6,7},{7,8},{8,9},{9,10},{10,1... | collective-permute-start | bytes 3145736 | tf_op jit(solution)/shard_map/ppermute | solution.py:15
  241.4 0.7 compare_and_fusion.2
  242.0 5.8 %collective-permute-start.6 = (bf16[1,128,512]{2,1,0:T(8,128)(2,1)S(1)}, bf16[1,128,512]{2,1,0:T(8,128)(2,1)S(1)}, u32[]{:S(2)}, u32[]{:S(2)}) collective-permute-start(bf16[1,128,512]{2,1,0:T(8,128)(2,1)S(1)} %copy-done.12), channel_id=1, source_target_pairs={{0,1},{1,2},{2,3},{3,4},{4,5},{5,6},{6,7},{7,8},{8,9},{9,10},{10,1... | collective-permute-start | bytes 393224 | tf_op jit(solution)/shard_map/ppermute | solution.py:15
  247.9 0.9 constant_dynamic-update-slice_fusion.4
  248.8 11.5 %collective-permute-done.6 = bf16[1,128,512]{2,1,0:T(8,128)(2,1)S(1)} collective-permute-done((bf16[1,128,512]{2,1,0:T(8,128)(2,1)S(1)}, bf16[1,128,512]{2,1,0:T(8,128)(2,1)S(1)}, u32[]{:S(2)}, u32[]{:S(2)}) %collective-permute-start.6) | collective-permute-done | bytes 131104 | tf_op jit(solution)/shard_map/ppermute | solution.py:15
  260.5 1.3 select_bitcast_fusion
  261.8 3.3 multiply_reduce_fusion.1
  265.1 0.1 copy.68
  265.2 0.6 copy.59
  265.8 0.3 copy-done.11
  266.1 1.2 multiply_reduce_fusion
  267.3 124.6 %psum.7 = f32[128]{0:T(128)S(1)} all-reduce(f32[128]{0:T(128)S(1)} %get-tuple-element.17), channel_id=1, replica_groups=mesh['dp'=16,'ctx'=32] {'dp','ctx'}, use_global_device_ids=true, to_apply=%region_8.9 | all-reduce | flops 128 | bytes 1024 | tf_op jit(solution)/shard_map/psum | solution.py:145
  391.9 0.5 broadcast_multiply_fusion.2
  392.4 4.2 %convert_bitcast_fusion = bf16[1,128,16,512]{3,1,2,0:T(8,128)(2,1)S(1)} fusion(bf16[16,128,512]{2,0,1:T(8,128)(2,1)} %all-gather.3.cloned.1.call-done, bf16[128,16,128]{2,1,0:T(8,128)(2,1)S(1)} %bitcast.248), kind=kOutput, calls=%fused_computation.10 | convolution fusion | flops 269484032 | bytes 4718592 | tf_op jit(solution)/shard_map/sthn,hnl->sthl/dot_general | solution.py:161
  396.6 0.5 fusion.91
  397.1 0.4 fusion.46
  397.5 0.5 fusion.90
  398.1 0.4 fusion.47
  398.5 2.4 fusion.34
  400.9 2.4 fusion.35
  403.3 1.1 copy.65
  (103 shorter events, 0.9 us)
Async XLA Ops:
  7.2 21.9 %copy-start.7 = (bf16[1,128,16,128]{3,2,1,0:T(8,128)(2,1)S(1)}, bf16[1,128,16,128]{3,2,1,0:T(8,128)(2,1)}, u32[]{:S(2)}) copy-start(bf16[1,128,16,128]{3,2,1,0:T(8,128)(2,1)} %param.15) | copy-start | bytes 1572868
  7.2 385.2 %all-gather.3.cloned.1.call-start = ((), (), s32[]{:S(2)}) async-start(), calls=%async_computation | async-start | bytes 2162688 | tf_op jit(solution)/shard_map/all_gather | solution.py:158
  7.2 241.6 %collective-permute-start.5 = (bf16[1,128,512]{2,1,0:T(8,128)(2,1)}, bf16[1,128,512]{2,1,0:T(8,128)(2,1)S(1)}, u32[]{:S(2)}, u32[]{:S(2)}) collective-permute-start(bf16[1,128,512]{2,1,0:T(8,128)(2,1)} %param.25), channel_id=1, source_target_pairs={{1,0},{2,1},{3,2},{4,3},{5,4},{6,5},{7,6},{8,7},{9,8},{10,9},{11,1... | collective-permute-start | bytes 393224 | tf_op jit(solution)/shard_map/ppermute | solution.py:15
  8.7 233.4 %collective-permute-start.4 = (bf16[1,128,512]{2,1,0:T(8,128)(2,1)}, bf16[1,128,512]{2,1,0:T(8,128)(2,1)}, u32[]{:S(2)}, u32[]{:S(2)}) collective-permute-start(bf16[1,128,512]{2,1,0:T(8,128)(2,1)} %param.25), channel_id=1, source_target_pairs={{2,0},{3,1},{4,2},{5,3},{6,4},{7,5},{8,6},{9,7},{10,8},{11,9},{12,... | collective-permute-start | bytes 393224 | tf_op jit(solution)/shard_map/ppermute | solution.py:15
  10.0 250.4 %collective-permute-start.7 = (bf16[1,128,512]{2,1,0:T(8,128)(2,1)}, bf16[1,128,512]{2,1,0:T(8,128)(2,1)S(1)}, u32[]{:S(2)}, u32[]{:S(2)}) collective-permute-start(bf16[1,128,512]{2,1,0:T(8,128)(2,1)} %param.25), channel_id=1, source_target_pairs={{0,2},{1,3},{2,4},{3,5},{4,6},{5,7},{6,8},{7,9},{8,10},{9,11},{10,... | collective-permute-start | bytes 393224 | tf_op jit(solution)/shard_map/ppermute | solution.py:15
  18.4 380.0 %all-gather.5.cloned.1.call-start = ((), (), s32[]{:S(2)}) async-start(), calls=%async_computation.1 | async-start | bytes 2162688 | tf_op jit(solution)/shard_map/all_gather | solution.py:159
  20.1 7.1 %copy-start.15 = (s32[1,64]{1,0:T(1,128)}, s32[1,64]{1,0:T(1,128)S(1)}, u32[]{:S(2)}) copy-start(s32[1,64]{1,0:T(1,128)S(1)} %get-tuple-element.29) | copy-start | bytes 772
  20.1 7.1 %copy-start.17 = (s32[1,64]{1,0:T(1,128)}, s32[1,64]{1,0:T(1,128)S(1)}, u32[]{:S(2)}) copy-start(s32[1,64]{1,0:T(1,128)S(1)} %get-tuple-element.30) | copy-start | bytes 772
  23.5 3.7 copy-start.30
  24.2 5.3 %copy-start.20 = (f32[2,64]{1,0:T(2,128)}, f32[2,64]{1,0:T(2,128)S(1)}, u32[]{:S(2)}) copy-start(f32[2,64]{1,0:T(2,128)S(1)} %get-tuple-element.38) | copy-start | bytes 1540
  30.8 1.5 copy-start.13
  194.4 1.5 copy-start.6
  194.4 1.6 copy-start.9
  195.9 2.1 copy-start.19
  197.9 3.7 copy-start
  201.5 8.0 %copy-start.2 = (f32[1,2,16,128,128]{4,3,2,1,0:T(8,128)}, f32[1,2,16,128,128]{4,3,2,1,0:T(8,128)S(1)}, u32[]{:S(2)}) copy-start(f32[1,2,16,128,128]{4,3,2,1,0:T(8,128)S(1)} %convolution_bitcast_fusion) | copy-start | bytes 6291460
  205.6 5.9 %copy-start.4 = (f32[1,2,16,128,128]{4,3,2,1,0:T(8,128)}, f32[1,2,16,128,128]{4,3,2,1,0:T(8,128)S(1)}, u32[]{:S(2)}) copy-start(f32[1,2,16,128,128]{4,3,2,1,0:T(8,128)S(1)} %subtract_bitcast_fusion) | copy-start | bytes 6291460
  207.6 9.0 %copy-start.8 = (bf16[1,128,16,128]{3,2,1,0:T(8,128)(2,1)S(1)}, bf16[1,128,16,128]{3,2,1,0:T(8,128)(2,1)}, u32[]{:S(2)}) copy-start(bf16[1,128,16,128]{3,2,1,0:T(8,128)(2,1)} %param.14) | copy-start | bytes 1572868
  207.6 9.8 %copy-start.22 = (s32[1,64]{1,0:T(1,128)S(1)}, s32[1,64]{1,0:T(1,128)}, u32[]{:S(2)}) copy-start(s32[1,64]{1,0:T(1,128)} %get-tuple-element.25) | copy-start | bytes 772
  207.6 9.8 %copy-start.23 = (s32[1,64]{1,0:T(1,128)S(1)}, s32[1,64]{1,0:T(1,128)}, u32[]{:S(2)}) copy-start(s32[1,64]{1,0:T(1,128)} %get-tuple-element.26) | copy-start | bytes 772
  207.6 9.8 %copy-start.24 = (s32[1,64]{1,0:T(1,128)S(1)}, s32[1,64]{1,0:T(1,128)}, u32[]{:S(2)}) copy-start(s32[1,64]{1,0:T(1,128)} %get-tuple-element.27) | copy-start | bytes 772
  207.6 9.8 %copy-start.25 = (s32[1,64]{1,0:T(1,128)S(1)}, s32[1,64]{1,0:T(1,128)}, u32[]{:S(2)}) copy-start(s32[1,64]{1,0:T(1,128)} %get-tuple-element.28) | copy-start | bytes 772
  207.6 9.8 %copy-start.26 = (s32[1,64]{1,0:T(1,128)S(1)}, s32[1,64]{1,0:T(1,128)}, u32[]{:S(2)}) copy-start(s32[1,64]{1,0:T(1,128)} %get-tuple-element.31) | copy-start | bytes 772
  207.7 9.8 %copy-start.27 = (s32[1,64]{1,0:T(1,128)S(1)}, s32[1,64]{1,0:T(1,128)}, u32[]{:S(2)}) copy-start(s32[1,64]{1,0:T(1,128)} %get-tuple-element.32) | copy-start | bytes 772
  207.7 20.5 %collective-permute-start.2 = (f32[1,16,128,128]{3,2,1,0:T(8,128)}, f32[1,16,128,128]{3,2,1,0:T(8,128)}, u32[]{:S(2)}, u32[]{:S(2)}) collective-permute-start(f32[1,16,128,128]{3,2,1,0:T(8,128)} %fusion.20), channel_id=1, source_target_pairs={{1,0},{2,1},{3,2},{4,3},{5,4},{6,5},{7,6},{8,7},{9,8},{10,9},{11,1... | collective-permute-start | bytes 3145736 | tf_op jit(solution)/shard_map/ppermute | solution.py:15
  211.6 21.5 %collective-permute-start = (f32[1,16,128,128]{3,2,1,0:T(8,128)}, f32[1,16,128,128]{3,2,1,0:T(8,128)}, u32[]{:S(2)}, u32[]{:S(2)}) collective-permute-start(f32[1,16,128,128]{3,2,1,0:T(8,128)} %fusion.22), channel_id=1, source_target_pairs={{0,1},{1,2},{2,3},{3,4},{4,5},{5,6},{6,7},{7,8},{8,9},{9,10},{10,1... | collective-permute-start | bytes 3145736 | tf_op jit(solution)/shard_map/ppermute | solution.py:15
  216.6 3.2 copy-start.28
  217.6 2.2 copy-start.18
  217.6 2.3 copy-start.1
  219.8 1.2 copy-start.21
  221.0 7.2 %copy-start.3 = (f32[1,2,16,128,128]{4,3,2,1,0:T(8,128)S(1)}, f32[1,2,16,128,128]{4,3,2,1,0:T(8,128)}, u32[]{:S(2)}) copy-start(f32[1,2,16,128,128]{4,3,2,1,0:T(8,128)} %copy-done.2) | copy-start | bytes 6291460
  221.0 7.2 %copy-start.5 = (f32[1,2,16,128,128]{4,3,2,1,0:T(8,128)S(1)}, f32[1,2,16,128,128]{4,3,2,1,0:T(8,128)}, u32[]{:S(2)}) copy-start(f32[1,2,16,128,128]{4,3,2,1,0:T(8,128)} %copy-done.4) | copy-start | bytes 6291460
  231.7 9.7 %copy-start.16 = (s32[1,64]{1,0:T(1,128)S(1)}, s32[1,64]{1,0:T(1,128)}, u32[]{:S(2)}) copy-start(s32[1,64]{1,0:T(1,128)} %copy-done.15) | copy-start | bytes 772
  231.7 9.7 %copy-start.29 = (s32[64]{0:T(128)S(1)}, s32[64]{0:T(128)}, u32[]{:S(2)}) copy-start(s32[64]{0:T(128)} %copy-done.28) | copy-start | bytes 772
  231.7 10.4 %copy-start.12 = (bf16[1,128,512]{2,1,0:T(8,128)(2,1)S(1)}, bf16[1,128,512]{2,1,0:T(8,128)(2,1)}, u32[]{:S(2)}) copy-start(bf16[1,128,512]{2,1,0:T(8,128)(2,1)} %param.25) | copy-start | bytes 393220
  231.7 28.8 %collective-permute-start.3 = (f32[1,16,128,128]{3,2,1,0:T(8,128)}, f32[1,16,128,128]{3,2,1,0:T(8,128)}, u32[]{:S(2)}, u32[]{:S(2)}) collective-permute-start(f32[1,16,128,128]{3,2,1,0:T(8,128)} %fusion.19), channel_id=1, source_target_pairs={{1,0},{2,1},{3,2},{4,3},{5,4},{6,5},{7,6},{8,7},{9,8},{10,9},{11,1... | collective-permute-start | bytes 3145736 | tf_op jit(solution)/shard_map/ppermute | solution.py:15
  235.5 26.3 %collective-permute-start.1 = (f32[1,16,128,128]{3,2,1,0:T(8,128)S(1)}, f32[1,16,128,128]{3,2,1,0:T(8,128)}, u32[]{:S(2)}, u32[]{:S(2)}) collective-permute-start(f32[1,16,128,128]{3,2,1,0:T(8,128)S(1)} %fusion.21), channel_id=1, source_target_pairs={{0,1},{1,2},{2,3},{3,4},{4,5},{5,6},{6,7},{7,8},{8,9},{9,10},{10,1... | collective-permute-start | bytes 3145736 | tf_op jit(solution)/shard_map/ppermute | solution.py:15
  242.0 18.3 %collective-permute-start.6 = (bf16[1,128,512]{2,1,0:T(8,128)(2,1)S(1)}, bf16[1,128,512]{2,1,0:T(8,128)(2,1)S(1)}, u32[]{:S(2)}, u32[]{:S(2)}) collective-permute-start(bf16[1,128,512]{2,1,0:T(8,128)(2,1)S(1)} %copy-done.12), channel_id=1, source_target_pairs={{0,1},{1,2},{2,3},{3,4},{4,5},{5,6},{6,7},{7,8},{8,9},{9,10},{10,1... | collective-permute-start | bytes 393224 | tf_op jit(solution)/shard_map/ppermute | solution.py:15
  265.1 1.0 copy-start.11
  265.1 1.0 copy-start.31
  265.2 127.2 %copy-start.10 = (bf16[1,128,16,128]{3,2,1,0:T(8,128)(2,1)S(1)}, bf16[1,128,16,128]{3,2,1,0:T(8,128)(2,1)}, u32[]{:S(2)}) copy-start(bf16[1,128,16,128]{3,2,1,0:T(8,128)(2,1)} %param.24) | copy-start | bytes 1572868
  396.6 0.9 copy-start.14
Sparse Core Ops, SparseCore 0:
  18.6 86.8 all-gather.2
  216.7 88.3 all-gather.4
where the time goes:
time: 417 us; the launch traced here: 411 us
  other arithmetic  174 us (42%)
  blocking collectives  125 us (30%)
  matrix products  41.3 us (10%)
  starting transfers between devices  29.7 us (7%)
  waiting for transfers between devices  17.3 us (4%)
  between operations  16.2 us (4%)
  local copies, waits for them, and re-layouts  8.72 us (2%)
    another operation x4, other arithmetic, block_maps(): jax.scipy.linalg.solve_triangular(identity_mat[None] + triangle, jnp.tran...  160 us
    psum x1, blocking collectives, shards(): total_grad = lax.psum(partial_grad, ('dp', 'ctx'))  125 us
    ppermute x8, starting transfers between devices, from_behind(): lax.ppermute(value, axis, [(source, source + steps) for source in range(l...  29.6 us
    ppermute x8, waiting for transfers between devices, from_behind(): lax.ppermute(value, axis, [(source, source + steps) for source in range(l...  17.3 us
    dot_general x4, matrix products, advance(): jnp.einsum('shcd,shdv->shcv', transfer_map, state, precision=exact_mode)  9.83 us
  transfers between devices with their start and end apart: 10, of which 2 were waited for; matrix products, arithmetic and copies ran while one was open for 53% of the time, Pallas kernels for 0%

commit v1 on v0

--- a/solution.py
+++ b/solution.py
@@ -7,6 +7,11 @@
 DOCBLK = 2
 DN = 128
 exact_mode = lax.Precision.HIGHEST
+
+
+def axis_by_axis(x, one, other):
+    middle = lax.psum(x, one)
+    return lax.psum(middle, other)
 
 
 def from_behind(value, axis, steps):
@@ -142,7 +147,7 @@
     normed = kda_raw * lax.rsqrt(meansq + 1e-06)
     kda_output = (normed * delta_norm_gain).astype(jnp.bfloat16)
     partial_grad = jnp.sum(normed * delta_output_cotangent.astype(jnp.float32), axis=(0, 1, 2))
-    total_grad = lax.psum(partial_grad, ("dp", "ctx"))
+    total_grad = axis_by_axis(partial_grad, "ctx", "dp")
     gain_grad = total_grad / math.sqrt(seqs * lax.axis_size("dp") * rows * ranks * heads)
     latent_width = compressed_latents.shape[2]
     neighbours = {0: compressed_latents}

time: 417 us -> 406 us (0.974)
  blocking collectives: 125 us -> 117 us
    psum x1 -> x2, blocking collectives: 125 us -> 117 us  [the longest x1 76.1 us: axis_by_axis(): middle = lax.psum(x, one)]
  transfers between devices with their start and end apart: 10 -> 10, of which waited for: 2 -> 2; matrix products, arithmetic and copies ran while one was open for 53% -> 54% of each run, Pallas kernels for 0% -> 0%
where the time goes in v1:
time: 406 us; the launch traced here: 403 us
  other arithmetic  174 us (43%)
  blocking collectives  117 us (29%)
  matrix products  41.3 us (10%)
  starting transfers between devices  29.5 us (7%)
  waiting for transfers between devices  17.1 us (4%)
  between operations  16.1 us (4%)
  local copies, waits for them, and re-layouts  8.74 us (2%)
    another operation x4, other arithmetic, block_maps(): jax.scipy.linalg.solve_triangular(identity_mat[None] + triangle, jnp.tran...  159 us
    psum x1, blocking collectives, axis_by_axis(): middle = lax.psum(x, one)  76.1 us
    psum x1, blocking collectives, axis_by_axis(): return lax.psum(middle, other)  41 us
    ppermute x8, starting transfers between devices, from_behind(): lax.ppermute(value, axis, [(source, source + steps) for source in range(l...  29.5 us
    ppermute x8, waiting for transfers between devices, from_behind(): lax.ppermute(value, axis, [(source, source + steps) for source in range(l...  17.1 us
    dot_general x4, matrix products, advance(): jnp.einsum('shcd,shdv->shcv', transfer_map, state, precision=exact_mode)  9.82 us
  transfers between devices with their start and end apart: 10, of which 2 were waited for; matrix products, arithmetic and copies ran while one was open for 54% of the time, Pallas kernels for 0%

profile of v1, /device:TPU:1, one launch (start us, length us, event | category | flops | bytes accessed | tf_op | source)
XLA Modules:
  0.0 403.4 jit_solution(15819941428707871163)
XLA Ops:
  7.2 1.4 collective-permute-start.5
  8.7 1.3 collective-permute-start.4
  10.0 7.0 %collective-permute-start.7 = (bf16[1,128,512]{2,1,0:T(8,128)(2,1)}, bf16[1,128,512]{2,1,0:T(8,128)(2,1)S(1)}, u32[]{:S(2)}, u32[]{:S(2)}) collective-permute-start(bf16[1,128,512]{2,1,0:T(8,128)(2,1)} %param.25), channel_id=1, source_target_pairs={{0,2},{1,3},{2,4},{3,5},{4,6},{5,7},{6,8},{7,9},{8,10},{9,11},{10,... | collective-permute-start | bytes 393224 | tf_op jit(solution)/shard_map/ppermute | solution.py:20
  16.9 1.5 copy.62
  18.6 1.5 broadcast_select_fusion.5
  20.1 0.2 slice_reduce_fusion
  20.3 0.7 iota_compare_fusion.5
  21.0 1.3 constant_dynamic-slice_fusion.7
  23.7 0.7 compare_convert_fusion
  24.4 0.7 multiply_reduce_fusion.2
  25.0 0.8 mul.321
  25.8 0.8 reshape.779
  26.7 0.7 neg.8
  27.4 0.8 mul.308
  28.2 1.1 convert.6
  29.3 0.3 fusion.36
  29.7 0.1 fusion.71
  29.8 0.9 fusion.42
  30.7 0.3 convert_multiply_fusion.2
  31.0 1.5 multiply_bitcast_fusion
  32.6 3.0 fusion.27
  35.6 158.7 %custom-call.4 = f32[1,2,16,1,64,64]{4,5,3,2,1,0:T(8,128)} custom-call(f32[1,2,16,1,64,64]{5,4,3,2,1,0:T(8,128)} %fusion.27), custom_call_target="InvertDiagBlocksLowerTriangular" | custom-call | tf_op jit(solution)/shard_map/vmap(vmap(jit(_solve_triangular)))/vmap()/triangular_solve | solution.py:46
  194.3 0.9 broadcast_compare_fusion
  195.2 0.2 fusion.77
  195.4 0.4 copy_multiply_fusion.1
  195.8 2.0 fusion.10
  197.9 3.6 convolution_bitcast_fusion
  201.5 4.0 subtract_bitcast_fusion
  205.6 2.0 fusion.20
  207.6 1.6 collective-permute-start.2
  209.3 2.0 fusion.22
  211.2 5.0 %collective-permute-start = (f32[1,16,128,128]{3,2,1,0:T(8,128)}, f32[1,16,128,128]{3,2,1,0:T(8,128)}, u32[]{:S(2)}, u32[]{:S(2)}) collective-permute-start(f32[1,16,128,128]{3,2,1,0:T(8,128)} %fusion.22), channel_id=1, source_target_pairs={{0,1},{1,2},{2,3},{3,4},{4,5},{5,6},{6,7},{7,8},{8,9},{9,10},{10,1... | collective-permute-start | bytes 3145736 | tf_op jit(solution)/shard_map/ppermute | solution.py:20
  216.3 0.3 fusion.37
  216.7 0.3 convert_multiply_fusion
  217.3 2.1 convolution_multiply_fusion.2
  219.4 0.1 compare_and_fusion.3
  219.5 1.1 fusion.45
  220.7 1.5 fusion.29
  222.1 6.0 %collective-permute-done.2 = f32[1,16,128,128]{3,2,1,0:T(8,128)} collective-permute-done((f32[1,16,128,128]{3,2,1,0:T(8,128)}, f32[1,16,128,128]{3,2,1,0:T(8,128)}, u32[]{:S(2)}, u32[]{:S(2)}) %collective-permute-start.2) | collective-permute-done | bytes 1048608 | tf_op jit(solution)/shard_map/ppermute | solution.py:20
  228.1 3.4 fusion.19
  231.6 1.4 collective-permute-start.3
  233.0 2.4 fusion.21
  235.4 5.9 %collective-permute-start.1 = (f32[1,16,128,128]{3,2,1,0:T(8,128)S(1)}, f32[1,16,128,128]{3,2,1,0:T(8,128)}, u32[]{:S(2)}, u32[]{:S(2)}) collective-permute-start(f32[1,16,128,128]{3,2,1,0:T(8,128)S(1)} %fusion.21), channel_id=1, source_target_pairs={{0,1},{1,2},{2,3},{3,4},{4,5},{5,6},{6,7},{7,8},{8,9},{9,10},{10,1... | collective-permute-start | bytes 3145736 | tf_op jit(solution)/shard_map/ppermute | solution.py:20
  241.3 0.7 compare_and_fusion.2
  242.0 5.9 %collective-permute-start.6 = (bf16[1,128,512]{2,1,0:T(8,128)(2,1)S(1)}, bf16[1,128,512]{2,1,0:T(8,128)(2,1)S(1)}, u32[]{:S(2)}, u32[]{:S(2)}) collective-permute-start(bf16[1,128,512]{2,1,0:T(8,128)(2,1)S(1)} %copy-done.12), channel_id=1, source_target_pairs={{0,1},{1,2},{2,3},{3,4},{4,5},{5,6},{6,7},{7,8},{8,9},{9,10},{10,1... | collective-permute-start | bytes 393224 | tf_op jit(solution)/shard_map/ppermute | solution.py:20
  247.8 0.9 constant_dynamic-update-slice_fusion.4
  248.8 11.1 %collective-permute-done.6 = bf16[1,128,512]{2,1,0:T(8,128)(2,1)S(1)} collective-permute-done((bf16[1,128,512]{2,1,0:T(8,128)(2,1)S(1)}, bf16[1,128,512]{2,1,0:T(8,128)(2,1)S(1)}, u32[]{:S(2)}, u32[]{:S(2)}) %collective-permute-start.6) | collective-permute-done | bytes 131104 | tf_op jit(solution)/shard_map/ppermute | solution.py:20
  260.0 1.3 select_bitcast_fusion
  261.4 3.3 multiply_reduce_fusion.1
  264.7 0.1 copy.68
  264.8 0.6 copy.59
  265.4 0.3 copy-done.11
  265.7 1.2 multiply_reduce_fusion
  266.9 76.1 %psum.14 = f32[128]{0:T(128)S(1)} all-reduce(f32[128]{0:T(128)S(1)} %get-tuple-element.17), channel_id=1, replica_groups=mesh['dp'=16,'ctx'=32] {'ctx'}, use_global_device_ids=true, to_apply=%region_8.9 | all-reduce | flops 128 | bytes 1024 | tf_op jit(solution)/shard_map/psum | solution.py:13
  343.0 41.0 %psum.15 = f32[128]{0:T(128)S(1)} all-reduce(f32[128]{0:T(128)S(1)} %psum.14), channel_id=1, replica_groups=mesh['dp'=16,'ctx'=32] {'dp'}, use_global_device_ids=true, to_apply=%region_9.10 | all-reduce | flops 128 | bytes 1024 | tf_op jit(solution)/shard_map/psum | solution.py:14
  383.9 0.5 broadcast_multiply_fusion.2
  384.5 4.2 %convert_bitcast_fusion = bf16[1,128,16,512]{3,1,2,0:T(8,128)(2,1)S(1)} fusion(bf16[16,128,512]{2,0,1:T(8,128)(2,1)} %all-gather.3.cloned.1.call-done, bf16[128,16,128]{2,1,0:T(8,128)(2,1)S(1)} %bitcast.248), kind=kOutput, calls=%fused_computation.10 | convolution fusion | flops 269484032 | bytes 4718592 | tf_op jit(solution)/shard_map/sthn,hnl->sthl/dot_general | solution.py:166
  388.6 0.5 fusion.91
  389.2 0.4 fusion.46
  389.6 0.5 fusion.90
  390.1 0.4 fusion.47
  390.6 2.4 fusion.34
  393.0 2.4 fusion.35
  395.4 1.1 copy.65
  (104 shorter events, 1.0 us)
Async XLA Ops:
  7.2 22.1 %copy-start.7 = (bf16[1,128,16,128]{3,2,1,0:T(8,128)(2,1)S(1)}, bf16[1,128,16,128]{3,2,1,0:T(8,128)(2,1)}, u32[]{:S(2)}) copy-start(bf16[1,128,16,128]{3,2,1,0:T(8,128)(2,1)} %param.15) | copy-start | bytes 1572868
  7.2 377.3 %all-gather.3.cloned.1.call-start = ((), (), s32[]{:S(2)}) async-start(), calls=%async_computation | async-start | bytes 2162688 | tf_op jit(solution)/shard_map/all_gather | solution.py:163
  7.2 241.5 %collective-permute-start.5 = (bf16[1,128,512]{2,1,0:T(8,128)(2,1)}, bf16[1,128,512]{2,1,0:T(8,128)(2,1)S(1)}, u32[]{:S(2)}, u32[]{:S(2)}) collective-permute-start(bf16[1,128,512]{2,1,0:T(8,128)(2,1)} %param.25), channel_id=1, source_target_pairs={{1,0},{2,1},{3,2},{4,3},{5,4},{6,5},{7,6},{8,7},{9,8},{10,9},{11,1... | collective-permute-start | bytes 393224 | tf_op jit(solution)/shard_map/ppermute | solution.py:20
  8.7 233.3 %collective-permute-start.4 = (bf16[1,128,512]{2,1,0:T(8,128)(2,1)}, bf16[1,128,512]{2,1,0:T(8,128)(2,1)}, u32[]{:S(2)}, u32[]{:S(2)}) collective-permute-start(bf16[1,128,512]{2,1,0:T(8,128)(2,1)} %param.25), channel_id=1, source_target_pairs={{2,0},{3,1},{4,2},{5,3},{6,4},{7,5},{8,6},{9,7},{10,8},{11,9},{12,... | collective-permute-start | bytes 393224 | tf_op jit(solution)/shard_map/ppermute | solution.py:20
  10.0 250.0 %collective-permute-start.7 = (bf16[1,128,512]{2,1,0:T(8,128)(2,1)}, bf16[1,128,512]{2,1,0:T(8,128)(2,1)S(1)}, u32[]{:S(2)}, u32[]{:S(2)}) collective-permute-start(bf16[1,128,512]{2,1,0:T(8,128)(2,1)} %param.25), channel_id=1, source_target_pairs={{0,2},{1,3},{2,4},{3,5},{4,6},{5,7},{6,8},{7,9},{8,10},{9,11},{10,... | collective-permute-start | bytes 393224 | tf_op jit(solution)/shard_map/ppermute | solution.py:20
  18.4 372.1 %all-gather.5.cloned.1.call-start = ((), (), s32[]{:S(2)}) async-start(), calls=%async_computation.1 | async-start | bytes 2162688 | tf_op jit(solution)/shard_map/all_gather | solution.py:164
  20.1 7.3 %copy-start.15 = (s32[1,64]{1,0:T(1,128)}, s32[1,64]{1,0:T(1,128)S(1)}, u32[]{:S(2)}) copy-start(s32[1,64]{1,0:T(1,128)S(1)} %get-tuple-element.29) | copy-start | bytes 772
  20.1 7.3 %copy-start.17 = (s32[1,64]{1,0:T(1,128)}, s32[1,64]{1,0:T(1,128)S(1)}, u32[]{:S(2)}) copy-start(s32[1,64]{1,0:T(1,128)S(1)} %get-tuple-element.30) | copy-start | bytes 772
  23.7 3.7 copy-start.30
  24.4 5.3 %copy-start.20 = (f32[2,64]{1,0:T(2,128)}, f32[2,64]{1,0:T(2,128)S(1)}, u32[]{:S(2)}) copy-start(f32[2,64]{1,0:T(2,128)S(1)} %get-tuple-element.38) | copy-start | bytes 1540
  31.0 1.5 copy-start.13
  194.3 1.5 copy-start.6
  194.3 1.6 copy-start.9
  195.8 2.1 copy-start.19
  197.8 3.7 copy-start
  201.5 7.8 %copy-start.2 = (f32[1,2,16,128,128]{4,3,2,1,0:T(8,128)}, f32[1,2,16,128,128]{4,3,2,1,0:T(8,128)S(1)}, u32[]{:S(2)}) copy-start(f32[1,2,16,128,128]{4,3,2,1,0:T(8,128)S(1)} %convolution_bitcast_fusion) | copy-start | bytes 6291460
  205.6 5.7 %copy-start.4 = (f32[1,2,16,128,128]{4,3,2,1,0:T(8,128)}, f32[1,2,16,128,128]{4,3,2,1,0:T(8,128)S(1)}, u32[]{:S(2)}) copy-start(f32[1,2,16,128,128]{4,3,2,1,0:T(8,128)S(1)} %subtract_bitcast_fusion) | copy-start | bytes 6291460
  207.6 8.8 %copy-start.8 = (bf16[1,128,16,128]{3,2,1,0:T(8,128)(2,1)S(1)}, bf16[1,128,16,128]{3,2,1,0:T(8,128)(2,1)}, u32[]{:S(2)}) copy-start(bf16[1,128,16,128]{3,2,1,0:T(8,128)(2,1)} %param.14) | copy-start | bytes 1572868
  207.6 9.5 %copy-start.22 = (s32[1,64]{1,0:T(1,128)S(1)}, s32[1,64]{1,0:T(1,128)}, u32[]{:S(2)}) copy-start(s32[1,64]{1,0:T(1,128)} %get-tuple-element.25) | copy-start | bytes 772
  207.6 9.5 %copy-start.23 = (s32[1,64]{1,0:T(1,128)S(1)}, s32[1,64]{1,0:T(1,128)}, u32[]{:S(2)}) copy-start(s32[1,64]{1,0:T(1,128)} %get-tuple-element.26) | copy-start | bytes 772
  207.6 9.5 %copy-start.24 = (s32[1,64]{1,0:T(1,128)S(1)}, s32[1,64]{1,0:T(1,128)}, u32[]{:S(2)}) copy-start(s32[1,64]{1,0:T(1,128)} %get-tuple-element.27) | copy-start | bytes 772
  207.6 9.5 %copy-start.25 = (s32[1,64]{1,0:T(1,128)S(1)}, s32[1,64]{1,0:T(1,128)}, u32[]{:S(2)}) copy-start(s32[1,64]{1,0:T(1,128)} %get-tuple-element.28) | copy-start | bytes 772
  207.6 9.5 %copy-start.26 = (s32[1,64]{1,0:T(1,128)S(1)}, s32[1,64]{1,0:T(1,128)}, u32[]{:S(2)}) copy-start(s32[1,64]{1,0:T(1,128)} %get-tuple-element.31) | copy-start | bytes 772
  207.6 9.5 %copy-start.27 = (s32[1,64]{1,0:T(1,128)S(1)}, s32[1,64]{1,0:T(1,128)}, u32[]{:S(2)}) copy-start(s32[1,64]{1,0:T(1,128)} %get-tuple-element.32) | copy-start | bytes 772
  207.6 20.5 %collective-permute-start.2 = (f32[1,16,128,128]{3,2,1,0:T(8,128)}, f32[1,16,128,128]{3,2,1,0:T(8,128)}, u32[]{:S(2)}, u32[]{:S(2)}) collective-permute-start(f32[1,16,128,128]{3,2,1,0:T(8,128)} %fusion.20), channel_id=1, source_target_pairs={{1,0},{2,1},{3,2},{4,3},{5,4},{6,5},{7,6},{8,7},{9,8},{10,9},{11,1... | collective-permute-start | bytes 3145736 | tf_op jit(solution)/shard_map/ppermute | solution.py:20
  211.2 21.7 %collective-permute-start = (f32[1,16,128,128]{3,2,1,0:T(8,128)}, f32[1,16,128,128]{3,2,1,0:T(8,128)}, u32[]{:S(2)}, u32[]{:S(2)}) collective-permute-start(f32[1,16,128,128]{3,2,1,0:T(8,128)} %fusion.22), channel_id=1, source_target_pairs={{0,1},{1,2},{2,3},{3,4},{4,5},{5,6},{6,7},{7,8},{8,9},{9,10},{10,1... | collective-permute-start | bytes 3145736 | tf_op jit(solution)/shard_map/ppermute | solution.py:20
  216.3 3.2 copy-start.28
  217.3 2.2 copy-start.18
  217.3 2.3 copy-start.1
  219.4 1.2 copy-start.21
  220.7 7.4 %copy-start.3 = (f32[1,2,16,128,128]{4,3,2,1,0:T(8,128)S(1)}, f32[1,2,16,128,128]{4,3,2,1,0:T(8,128)}, u32[]{:S(2)}) copy-start(f32[1,2,16,128,128]{4,3,2,1,0:T(8,128)} %copy-done.2) | copy-start | bytes 6291460
  220.7 7.4 %copy-start.5 = (f32[1,2,16,128,128]{4,3,2,1,0:T(8,128)S(1)}, f32[1,2,16,128,128]{4,3,2,1,0:T(8,128)}, u32[]{:S(2)}) copy-start(f32[1,2,16,128,128]{4,3,2,1,0:T(8,128)} %copy-done.4) | copy-start | bytes 6291460
  231.6 9.7 %copy-start.16 = (s32[1,64]{1,0:T(1,128)S(1)}, s32[1,64]{1,0:T(1,128)}, u32[]{:S(2)}) copy-start(s32[1,64]{1,0:T(1,128)} %copy-done.15) | copy-start | bytes 772
  231.6 9.7 %copy-start.29 = (s32[64]{0:T(128)S(1)}, s32[64]{0:T(128)}, u32[]{:S(2)}) copy-start(s32[64]{0:T(128)} %copy-done.28) | copy-start | bytes 772
  231.6 10.4 %copy-start.12 = (bf16[1,128,512]{2,1,0:T(8,128)(2,1)S(1)}, bf16[1,128,512]{2,1,0:T(8,128)(2,1)}, u32[]{:S(2)}) copy-start(bf16[1,128,512]{2,1,0:T(8,128)(2,1)} %param.25) | copy-start | bytes 393220
  231.6 28.5 %collective-permute-start.3 = (f32[1,16,128,128]{3,2,1,0:T(8,128)}, f32[1,16,128,128]{3,2,1,0:T(8,128)}, u32[]{:S(2)}, u32[]{:S(2)}) collective-permute-start(f32[1,16,128,128]{3,2,1,0:T(8,128)} %fusion.19), channel_id=1, source_target_pairs={{1,0},{2,1},{3,2},{4,3},{5,4},{6,5},{7,6},{8,7},{9,8},{10,9},{11,1... | collective-permute-start | bytes 3145736 | tf_op jit(solution)/shard_map/ppermute | solution.py:20
  235.4 26.0 %collective-permute-start.1 = (f32[1,16,128,128]{3,2,1,0:T(8,128)S(1)}, f32[1,16,128,128]{3,2,1,0:T(8,128)}, u32[]{:S(2)}, u32[]{:S(2)}) collective-permute-start(f32[1,16,128,128]{3,2,1,0:T(8,128)S(1)} %fusion.21), channel_id=1, source_target_pairs={{0,1},{1,2},{2,3},{3,4},{4,5},{5,6},{6,7},{7,8},{8,9},{9,10},{10,1... | collective-permute-start | bytes 3145736 | tf_op jit(solution)/shard_map/ppermute | solution.py:20
  242.0 18.0 %collective-permute-start.6 = (bf16[1,128,512]{2,1,0:T(8,128)(2,1)S(1)}, bf16[1,128,512]{2,1,0:T(8,128)(2,1)S(1)}, u32[]{:S(2)}, u32[]{:S(2)}) collective-permute-start(bf16[1,128,512]{2,1,0:T(8,128)(2,1)S(1)} %copy-done.12), channel_id=1, source_target_pairs={{0,1},{1,2},{2,3},{3,4},{4,5},{5,6},{6,7},{7,8},{8,9},{9,10},{10,1... | collective-permute-start | bytes 393224 | tf_op jit(solution)/shard_map/ppermute | solution.py:20
  264.6 1.0 copy-start.11
  264.7 1.0 copy-start.31
  264.8 119.7 %copy-start.10 = (bf16[1,128,16,128]{3,2,1,0:T(8,128)(2,1)S(1)}, bf16[1,128,16,128]{3,2,1,0:T(8,128)(2,1)}, u32[]{:S(2)}) copy-start(bf16[1,128,16,128]{3,2,1,0:T(8,128)(2,1)} %param.24) | copy-start | bytes 1572868
  388.6 1.0 copy-start.14
Sparse Core Ops, SparseCore 0:
  18.6 86.6 all-gather.2
  216.4 88.7 all-gather.4
